TPU v7x, 256 devices: a whole 4x4x8 slice. The times are simulated.
256 devices in a mesh: seq: 16 (over x_hi, y, core), heads: 16 (over z, x_lo).
Axes of the slice: x: 4 (x_hi: 2, x_lo: 2; x = x_hi * 2 + x_lo), y: 4, z: 8, core: 2. Of those that a mesh axis runs over, the one named last changes fastest.
Arguments:
- activations: bfloat16 [12288, 4096], P('seq', 'heads'), may hold values from -24 to 24
- w_query: bfloat16 [4096, 4096], P(None, 'heads'), may hold values from -0.1875 to 0.1875
- w_key: bfloat16 [4096, 4096], P(None, 'heads'), may hold values from -0.09375 to 0.09375
- w_value: bfloat16 [4096, 4096], P(None, 'heads'), may hold values from -0.09375 to 0.09375
- w_out: bfloat16 [4096, 4096], P('heads'), may hold values from -0.1875 to 0.1875
- windows: int32 [32], P('heads'), may hold values from 1 to 2, as said below
- rand_blocks: int32 [96, 3], P('seq'), may hold values from 0 to 95, as said below
- global_pos: int32 [128], replicated, may hold values from 0 to 12287, as said below
Outputs:
- attended: bfloat16 [12288, 4096], P('seq', 'heads')
Inputs may be any that keep to these rules, and one draw needn't show every extreme that they name: `windows`: some head has reach 2. `rand_blocks`: the 3 entries of a row are distinct. Of the 18 entries in the rows of one index of seq, at most 2 fall into the 6 blocks of any one index, and exactly 2 into those of some index. `global_pos`: Distinct. At most 32 fall into the 768 positions of one index of seq, and exactly 32 into those of some index.
All inputs are finite; a program needn't handle non-finite values.
Results may differ from a plain program's by a relative error of at most 0.024.
The roundings to bfloat16 on the way count: a program that leaves them out, or rounds other values in their place, can miss the bound.
Values may be sent and summed in bfloat16 or wider, within the bound.
No kernel may reach another device: no remote copies, remote signals or barrier semaphores. Data moves between devices by JAX's collectives and lax.ppermute only.
A program may use at most 128 MiB of HBM per device.

v0:
```python
import math
import jax
import jax.numpy as jnp
from jax import lax
from jax.sharding import PartitionSpec as P

WMAX = 2
NEGATIVE = -1e30


def extended(block, sides, width):
    for axis, dim in sides:
        count = lax.axis_size(axis)
        forward = [(i, i + 1) for i in range(count - 1)]
        forward.append((count - 1, 0))
        backward = [(target, source) for source, target in forward]
        low = lax.ppermute(
            lax.slice_in_dim(block, block.shape[dim] - width, None, axis=dim), axis, forward
        )
        high = lax.ppermute(lax.slice_in_dim(block, 0, width, axis=dim), axis, backward)
        block = jnp.concatenate([low, block, high], axis=dim)
    return block


def combined_all(value, axis, join):
    pieces = jax.tree.map(lambda part: lax.all_gather(part, axis), value)
    head = jax.tree.map(lambda part: part[0], pieces)
    tail = jax.tree.map(lambda part: part[1:], pieces)
    running, _ = lax.scan(lambda running, slab: (join(running, slab), None), head, tail)
    return running


def fold_scores(state, scores, valid):
    top_old, sum_old, acc_old = state
    masked = jnp.where(valid, scores, NEGATIVE)
    top_new = jnp.maximum(top_old, jnp.max(masked, axis=-1))
    probs = jnp.where(valid, jnp.exp(masked - top_new[..., None]), 0.0)
    keep = jnp.exp(top_old - top_new)
    return (
        top_new,
        keep * sum_old + jnp.sum(probs, axis=-1),
        keep[..., None] * acc_old,
        probs.astype(jnp.bfloat16),
    )


def join_states(first, second):
    top_first, sum_first, acc_first = first
    top_second, sum_second, acc_second = second
    top_both = jnp.maximum(top_first, top_second)
    keep_first = jnp.exp(top_first - top_both)
    keep_second = jnp.exp(top_second - top_both)
    return (
        top_both,
        keep_first * sum_first + keep_second * sum_second,
        keep_first[..., None] * acc_first + keep_second[..., None] * acc_second,
    )


def on_device(activations, w_query, w_key, w_value, w_out, windows, rand_blocks, global_pos):
    rows_here = activations.shape[0]
    group_width = w_query.shape[1]
    heads_here = windows.shape[0]
    head_size = group_width // heads_here
    blocks_here = rand_blocks.shape[0]
    block_rows = rows_here // blocks_here
    picks_per_block = rand_blocks.shape[1]
    seq_count = lax.axis_size("seq")
    position = lax.axis_index("seq")
    score_scale = 1.0 / math.sqrt(head_size)
    piece = lax.all_gather(activations, "heads", axis=1, tiled=True)
    sums_query = jnp.dot(piece, w_query, preferred_element_type=jnp.float32)
    sums_key = jnp.dot(piece, w_key, preferred_element_type=jnp.float32)
    sums_value = jnp.dot(piece, w_value, preferred_element_type=jnp.float32)
    query = sums_query.astype(jnp.bfloat16)
    keys = sums_key.astype(jnp.bfloat16)
    values = sums_value.astype(jnp.bfloat16)
    query_blocks = query.reshape(blocks_here, block_rows, heads_here, head_size)
    stacked = jnp.stack([keys, values], 0)
    padded = extended(stacked, (("seq", 1),), WMAX * block_rows)
    span = 2 * WMAX + 1
    padded_blocks = padded.reshape(2, blocks_here + 2 * WMAX, block_rows, heads_here, head_size)
    window_kv = jnp.concatenate(
        [padded_blocks[:, offset : offset + blocks_here, None] for offset in range(span)], axis=2
    )
    window_kv = window_kv.reshape(2, blocks_here, span * block_rows, heads_here, head_size)
    distance = jnp.abs(jnp.arange(span, dtype=jnp.int32) - WMAX)
    window_valid = jnp.repeat(distance[None, :] <= windows[:, None], block_rows, axis=1)[
        None, :, None, :
    ]
    scores = (
        jnp.einsum(
            "bqhd,bkhd->bhqk", query_blocks, window_kv[0], preferred_element_type=jnp.float32
        )
        * score_scale
    )
    start_state = (
        jnp.full((blocks_here, heads_here, block_rows), NEGATIVE, jnp.float32),
        jnp.zeros((blocks_here, heads_here, block_rows), jnp.float32),
        jnp.zeros((blocks_here, heads_here, block_rows, head_size), jnp.float32),
    )
    top, total, accum, attention_weights = fold_scores(start_state, scores, window_valid)
    accum = jnp.einsum(
        "bhqk,bkhd->bhqd", attention_weights, window_kv[1], preferred_element_type=jnp.float32
    )
    state = (top, total, accum)
    all_valid = jnp.ones((1, 1, 1, 1), dtype=bool)
    targets = rand_blocks.reshape(-1)
    request_count = targets.shape[0]
    sources = targets // blocks_here
    order = jnp.arange(request_count, dtype=jnp.int32)
    earlier = (sources[:, None] == sources[None, :]) & (order[None, :] < order[:, None])
    ranks = jnp.sum(earlier.astype(jnp.int32), axis=1)
    slot_count = (request_count + seq_count - 1) // seq_count
    hits = (sources[:, None, None] == jnp.arange(seq_count, dtype=jnp.int32)[None, :, None]) & (
        ranks[:, None, None] == jnp.arange(slot_count, dtype=jnp.int32)[None, None, :]
    )
    slot_request = jnp.sum(jnp.where(hits, order[:, None, None], 0), axis=0)
    slot_live = jnp.any(hits, axis=0)
    row_steps = jnp.arange(block_rows, dtype=jnp.int32)
    owner_ids = jnp.arange(blocks_here, dtype=jnp.int32)
    piece = lax.all_gather(stacked, "seq", axis=1, tiled=True)
    count = piece.shape[1]
    picked = slot_request.reshape(-1)
    alive = slot_live.reshape(-1)
    slot_total = picked.shape[0]
    offset_rows = targets[picked][:, None] * block_rows + row_steps[None, :]
    chosen = piece[:, jnp.clip(offset_rows, 0, count - 1).reshape(-1)]
    chosen = chosen.reshape(2, slot_total * block_rows, heads_here, head_size)
    part_scores = (
        jnp.einsum("bqhd,khd->bhqk", query_blocks, chosen[0], preferred_element_type=jnp.float32)
        * score_scale
    )
    belongs = alive[None, :] & ((picked // picks_per_block)[None, :] == owner_ids[:, None])
    valid = jnp.repeat(belongs, block_rows, axis=1)[:, None, None, :]
    top_new, total_new, accum_new, part_weights = fold_scores(state, part_scores, valid)
    state = (
        top_new,
        total_new,
        accum_new
        + jnp.einsum("bhqk,khd->bhqd", part_weights, chosen[1], preferred_element_type=jnp.float32),
    )
    global_count = global_pos.shape[0]
    local_pos = global_pos - position * rows_here
    owned = (local_pos >= 0) & (local_pos < rows_here)
    row_ids = jnp.arange(rows_here, dtype=jnp.int32)
    selector = owned[:, None] & (local_pos[:, None] == row_ids[None, :])
    projected = jnp.concatenate([query, keys, values], axis=1)
    chosen_rows = jnp.dot(
        selector.astype(jnp.bfloat16), projected, preferred_element_type=jnp.float32
    )
    shared = lax.psum(chosen_rows.astype(jnp.bfloat16), "seq")
    g_query = shared[:, :group_width].reshape(global_count, heads_here, head_size)
    g_key = shared[:, group_width : 2 * group_width].reshape(global_count, heads_here, head_size)
    g_value = shared[:, 2 * group_width :].reshape(global_count, heads_here, head_size)
    global_score_rows = (
        jnp.einsum("bqhd,ghd->bhqg", query_blocks, g_key, preferred_element_type=jnp.float32)
        * score_scale
    )
    top, total, accum, attention_weights = fold_scores(state, global_score_rows, all_valid)
    accum = accum + jnp.einsum(
        "bhqg,ghd->bhqd", attention_weights, g_value, preferred_element_type=jnp.float32
    )
    sparse = (accum / total[..., None]).transpose(0, 2, 1, 3).reshape(rows_here, group_width)
    key_heads = keys.reshape(rows_here, heads_here, head_size)
    value_heads = values.reshape(rows_here, heads_here, head_size)
    g_scores = (
        jnp.einsum("ghd,thd->hgt", g_query, key_heads, preferred_element_type=jnp.float32)
        * score_scale
    )
    g_top = jnp.max(g_scores, axis=-1)
    g_probs = jnp.exp(g_scores - g_top[..., None])
    g_total = jnp.sum(g_probs, axis=-1)
    g_accum = jnp.einsum(
        "hgt,thd->hgd",
        g_probs.astype(jnp.bfloat16),
        value_heads,
        preferred_element_type=jnp.float32,
    )
    merged_top, merged_total, merged_accum = combined_all(
        (g_top, g_total, g_accum), "seq", join_states
    )
    finished = merged_accum / merged_total[..., None]
    placing = selector.astype(jnp.float32).T
    placed = jnp.einsum("tg,hgd->thd", placing, finished, precision=lax.Precision.HIGHEST)
    is_global = jnp.sum(placing, axis=1) > 0.5
    context = jnp.where(is_global[:, None], placed.reshape(rows_here, group_width), sparse).astype(
        jnp.bfloat16
    )
    term = jnp.dot(context, w_out, preferred_element_type=jnp.float32)
    return lax.psum_scatter(term.astype(jnp.bfloat16), "heads", scatter_dimension=1, tiled=True)


def solution(mesh):
    in_specs = (
        P("seq", "heads"),
        P(None, "heads"),
        P(None, "heads"),
        P(None, "heads"),
        P("heads", None),
        P("heads"),
        P("seq", None),
        P(),
    )
    out_specs = P("seq", "heads")
    return jax.shard_map(
        on_device, mesh=mesh, in_specs=in_specs, out_specs=out_specs, check_vma=False
    )
```

profile of v0, /device:TPU:1, one launch (start us, length us, event | category | flops | bytes accessed | tf_op | source)
XLA Modules:
  0.0 761.6 jit_solution(3525437572789591166)
XLA Ops:
  8.0 157.4 %all-gather.9.cloned.1.call-done = bf16[768,4096]{1,0:T(8,128)(2,1)} async-done(((bf16[768,256]{1,0:T(8,128)(2,1)}), bf16[768,4096]{1,0:T(8,128)(2,1)}) %all-gather.9.cloned.1.call-update) | async-done | bytes 6291472 | tf_op jit(solution)/shard_map/all_gather | solution.py:71
  165.4 5.4 convolution_convert_fusion.1
  176.5 143.8 %all-reduce.2.cloned.1.call-done = bf16[128,768]{1,0:T(8,128)(2,1)} async-done(((bf16[128,768]{1,0:T(8,128)(2,1)}), bf16[128,768]{1,0:T(8,128)(2,1)}) %all-reduce.2.cloned.1.call-update) | async-done | bytes 196624 | tf_op jit(solution)/shard_map/psum | solution.py:152
  339.5 26.6 %all-gather.3 = f32[16,2,128]{2,1,0:T(2,128)S(1)} all-gather(f32[1,2,128]{2,1,0:T(2,128)S(1)} %bitcast.208), channel_id=2, replica_groups=mesh['seq'=16,'heads'=16] {'seq'}, dimensions={0}, use_global_device_ids=true | all-gather | bytes 17408 | tf_op jit(solution)/shard_map/all_gather | solution.py:26
  366.4 19.3 %all-gather.4 = f32[16,2,128]{2,1,0:T(2,128)S(1)} all-gather(f32[1,2,128]{2,1,0:T(2,128)S(1)} %bitcast.209), channel_id=3, replica_groups=mesh['seq'=16,'heads'=16] {'seq'}, dimensions={0}, use_global_device_ids=true | all-gather | bytes 17408 | tf_op jit(solution)/shard_map/all_gather | solution.py:26
  390.8 2.3 pad_maximum_fusion
  393.1 2.5 copy.143
  395.6 3.0 reshape.310
  402.2 4.7 fusion.94
  409.2 2.7 fusion.8
  411.9 3.0 slice.104
  415.0 16.8 %while.14 = (s32[]{:T(128)}, f32[2,128]{1,0:T(2,128)S(1)}, f32[2,128]{1,0:T(2,128)S(1)}, f32[2,128,128]{2,1,0:T(8,128)S(1)}, f32[15,2,128]{2,1,0:T(2,128)S(1)}, ...) while((s32[]{:T(128)}, f32[2,128]{1,0:T(2,128)S(1)}, f32[2,128]{1,0:T(2,128)S(1)}, ...), condition=%wide.region_5.6_spmd, body=%wide.region_4.5_spmd.sunk | while | flops 99842 | bytes 403557 | solution.py:29
  432.0 45.2 %all-gather.11.cloned.1.call-done = bf16[2,12288,256]{1,2,0:T(8,128)(2,1)} async-done(((bf16[2,768,256]{1,2,0:T(8,128)(2,1)}), bf16[2,12288,256]{1,2,0:T(8,128)(2,1)}) %all-gather.11.cloned.1.call-update) | async-done | bytes 12582928 | tf_op jit(solution)/shard_map/all_gather | solution.py:122
  477.2 30.9 %copy.151 = bf16[2,12288,256]{2,0,1:T(2,128)(2,1)} copy(bf16[2,12288,256]{1,2,0:T(8,128)(2,1)} %all-gather.11.cloned.1.call-done) | data formatting | bytes 25165824 | tf_op jit(solution)/shard_map/all_gather | solution.py:122
  508.2 37.2 %gather_fusion.1 = bf16[4096,2,256]{2,1,0:T(2,128)(2,1)} fusion(bf16[2,12288,256]{2,0,1:T(2,128)(2,1)} %copy.151, s32[4096]{0:T(1024)S(1)} %copy-done.8), kind=kCustom, calls=%fused_computation.1 | custom fusion | bytes 8404992 | tf_op jit(solution)/shard_map/gather | solution.py:128
  545.3 9.9 %fusion.93 = (bf16[1,4096,256]{2,0,1:T(2,128)(2,1)}, bf16[1,4096,256]{2,0,1:T(2,128)(2,1)}) fusion(bf16[2,4096,256]{2,0,1:T(2,128)(2,1)} %bitcast.183), kind=kLoop, calls=%fused_computation.149 | loop fusion | bytes 8388608 | tf_op jit(solution)/shard_map/slice | solution.py:131
  555.2 9.8 %copy.152 = bf16[1,4096,256]{1,2,0:T(8,128)(2,1)} copy(bf16[1,4096,256]{2,0,1:T(2,128)(2,1)} %get-tuple-element.72) | data formatting | bytes 4194304 | tf_op jit(solution)/shard_map/slice | solution.py:131
  565.0 9.8 %copy.160 = bf16[1,4096,256]{1,2,0:T(8,128)(2,1)} copy(bf16[1,4096,256]{2,0,1:T(2,128)(2,1)} %get-tuple-element.73) | data formatting | bytes 4194304 | tf_op jit(solution)/shard_map/slice | solution.py:141
  574.8 7.7 %fusion.3 = (f32[6,2,128]{2,0,1:T(8,128)S(1)}, f32[2,4096,6,128]{3,1,2,0:T(8,128)S(1)}) fusion(pred[6,4096]{1,0:T(8,128)(4,1)S(1)} %bitcast.199, bf16[4096,2,128,1]{0,2,3,1:T(8,128)(2,1)} %bitcast.195, bf16[6,128,2,128]{3,2,1,0:T(2,128)(2,1)S(1)} %copy-done.3), kind=kOutput, calls=%fused_computation.13 | convolution fusion | flops 1629485568 | bytes 27686912 | tf_op jit(solution)/shard_map/bqhd,khd->bhqk/dot_general | solution.py:131
  583.9 13.8 %fusion.4 = (f32[6,2,128]{2,0,1:T(8,128)S(1)}, bf16[6,2,128,4096]{2,3,0,1:T(8,128)(2,1)}) fusion(f32[2,4096,6,128]{3,1,2,0:T(8,128)S(1)} %get-tuple-element.89, f32[6,2,128]{2,0,1:T(8,128)S(1)} %copy.162, pred[6,4096]{1,0:T(8,128)(4,1)S(1)} %bitcast.200), kind=kLoop, calls=%fused_computation.14 | loop fusion | flops 37747200 | bytes 37785600 | tf_op jit(solution)/shard_map/reduce_sum | solution.py:41
  597.7 10.6 %fusion.18 = f32[6,128,2,128]{3,1,2,0:T(8,128)} fusion(bf16[4096,2,128,1]{0,2,1,3:T(8,128)(2,1)S(1)} %bitcast.194, bf16[6,2,128,4096]{2,3,0,1:T(8,128)(2,1)} %get-tuple-element.71), kind=kOutput, calls=%fused_computation.31 | convolution fusion | flops 1610612736 | bytes 15466496 | tf_op jit(solution)/shard_map/bhqk,khd->bhqd/dot_general | solution.py:141
  608.3 3.2 fusion.33
  613.0 4.5 convolution_convert_fusion
  617.5 137.5 %reduce-scatter.2.cloned.1.call-done = bf16[768,256]{1,0:T(8,128)(2,1)} async-done(((bf16[768,4096]{1,0:T(8,128)(2,1)}), bf16[768,256]{1,0:T(8,128)(2,1)}) %reduce-scatter.2.cloned.1.call-update) | async-done | bytes 393232 | tf_op jit(solution)/shard_map/reduce_scatter | solution.py:191
  (169 shorter events, 57.1 us)
Async XLA Ops:
  6.5 606.5 %copy-start = (bf16[256,4096]{1,0:T(8,128)(2,1)S(1)}, bf16[256,4096]{1,0:T(8,128)(2,1)}, u32[]{:S(2)}) copy-start(bf16[256,4096]{1,0:T(8,128)(2,1)} %param.14) | copy-start | bytes 6291460
  6.5 158.8 %all-gather.9.cloned.1.call-start = ((), (), s32[]{:S(2)}) async-start(), calls=%async_computation.1 | async-start | bytes 6684672 | tf_op jit(solution)/shard_map/all_gather | solution.py:71
  7.3 313.1 %all-reduce.2.cloned.1.call-start = ((), (), s32[]{:S(2)}) async-start(), calls=%async_computation.2 | async-start | bytes 393216 | tf_op jit(solution)/shard_map/psum | solution.py:152
  8.0 322.1 %copy-start.15 = (pred[128]{0:T(512)(128)(4,1)}, pred[128]{0:T(512)(128)(4,1)S(1)}, u32[]{:S(2)}) copy-start(pred[128]{0:T(512)(128)(4,1)S(1)} %get-tuple-element.68) | copy-start | bytes 388
  8.0 322.1 %copy-start.17 = (s32[128]{0:T(128)}, s32[128]{0:T(128)S(1)}, u32[]{:S(2)}) copy-start(s32[128]{0:T(128)S(1)} %get-tuple-element.69) | copy-start | bytes 1540
  165.4 5.4 copy-start.20
  165.4 5.8 copy-start.21
  175.2 146.7 %copy-start.6 = (bf16[768,256]{0,1:T(8,128)(2,1)}, bf16[768,256]{0,1:T(8,128)(2,1)S(1)}, u32[]{:S(2)}) copy-start(bf16[768,256]{0,1:T(8,128)(2,1)S(1)} %convolution_convert_fusion.3) | copy-start | bytes 1179652
  175.2 151.2 %copy-start.23 = (s32[2]{0:T(128)S(1)}, s32[2]{0:T(128)}, u32[]{:S(2)}) copy-start(s32[2]{0:T(128)} %param.15) | copy-start | bytes 28
  175.2 151.9 %copy-start.14 = (s32[6,3]{0,1:T(4,128)S(1)}, s32[6,3]{0,1:T(4,128)}, u32[]{:S(2)}) copy-start(s32[6,3]{0,1:T(4,128)} %param.16) | copy-start | bytes 220
  176.5 235.4 %all-gather.13.cloned.1.call-start = ((), (), s32[]{:S(2)}) async-start(), calls=%async_computation.5 | async-start | bytes 2228224 | tf_op jit(solution)/shard_map/all_gather | solution.py:26
  324.3 152.9 %all-gather.11.cloned.1.call-start = ((), (), s32[]{:S(2)}) async-start(), calls=%async_computation.3 | async-start | bytes 13369344 | tf_op jit(solution)/shard_map/all_gather | solution.py:122
  326.3 428.7 %reduce-scatter.2.cloned.1.call-start = ((), (), s32[]{:S(2)}) async-start(), calls=%async_computation.4 | async-start | bytes 6684672 | tf_op jit(solution)/shard_map/reduce_scatter | solution.py:191
  337.0 53.8 %collective-permute-start = (bf16[2,256,256]{1,2,0:T(8,128)(2,1)}, bf16[2,256,256]{1,2,0:T(8,128)(2,1)S(1)}, u32[]{:S(2)}, u32[]{:S(2)}) collective-permute-start(bf16[2,256,256]{1,2,0:T(8,128)(2,1)} %get-tuple-element.78), channel_id=1, source_target_pairs={{0,16},{16,32},{32,48},{48,64},{64,80},{80,96},{96,112},{112,128},... | collective-permute-start | bytes 786440 | tf_op jit(solution)/shard_map/ppermute | solution.py:17
  337.5 53.3 %collective-permute-start.1 = (bf16[2,256,256]{1,2,0:T(8,128)(2,1)}, bf16[2,256,256]{1,2,0:T(8,128)(2,1)}, u32[]{:S(2)}, u32[]{:S(2)}) collective-permute-start(bf16[2,256,256]{1,2,0:T(8,128)(2,1)} %get-tuple-element.79), channel_id=1, source_target_pairs={{16,0},{32,16},{48,32},{64,48},{80,64},{96,80},{112,96},{128,112},... | collective-permute-start | bytes 786440 | tf_op jit(solution)/shard_map/ppermute | solution.py:20
  366.1 20.1 %copy-start.10 = (f32[16,2,128]{2,1,0:T(2,128)}, f32[16,2,128]{2,1,0:T(2,128)S(1)}, u32[]{:S(2)}) copy-start(f32[16,2,128]{2,1,0:T(2,128)S(1)} %all-gather.3) | copy-start | bytes 49156
  409.2 5.8 slice-start.1
  409.2 5.8 slice-start.2
  409.2 5.8 copy-start.12
  432.0 76.1 %copy-start.8 = (s32[4096]{0:T(1024)S(1)}, s32[4096]{0:T(1024)}, u32[]{:S(2)}) copy-start(s32[4096]{0:T(1024)} %broadcast_clamp_fusion) | copy-start | bytes 49156
  565.0 9.8 %copy-start.7 = (pred[1,6,32,128]{3,1,2,0:T(8,128)(4,1)S(1)}, pred[1,6,32,128]{3,1,2,0:T(8,128)(4,1)}, u32[]{:S(2)}) copy-start(pred[1,6,32,128]{3,1,2,0:T(8,128)(4,1)} %copy.235) | copy-start | bytes 73732
  574.8 7.8 %copy-start.4 = (f32[6,2,128,128]{2,3,0,1:T(8,128)S(1)}, f32[6,2,128,128]{2,3,0,1:T(8,128)}, u32[]{:S(2)}) copy-start(f32[6,2,128,128]{2,3,0,1:T(8,128)} %get-tuple-element.87) | copy-start | bytes 2359300
  574.8 7.9 %copy-start.1 = (f32[6,2,128,640]{3,2,1,0:T(8,128)S(1)}, f32[6,2,128,640]{3,2,1,0:T(8,128)}, u32[]{:S(2)}) copy-start(f32[6,2,128,640]{3,2,1,0:T(8,128)} %get-tuple-element.91) | copy-start | bytes 11796484
  583.9 13.8 %copy-start.5 = (bf16[1,4096,256]{1,2,0:T(8,128)(2,1)S(1)}, bf16[1,4096,256]{1,2,0:T(8,128)(2,1)}, u32[]{:S(2)}) copy-start(bf16[1,4096,256]{1,2,0:T(8,128)(2,1)} %copy.160) | copy-start | bytes 6291460
  (10 other events, 18.1 us)
Sparse Core Ops, SparseCore 0:
  9.1 156.2 all-gather.8
  176.6 143.6 all-reduce.1
  324.4 55.9 all-gather.12
  383.3 93.8 all-gather.10
  617.7 137.3 reduce-scatter.1
where the time goes:
time: 764 us; the launch traced here: 762 us
  waiting for transfers between devices  485 us (63%)
  local copies, waits for them, and re-layouts  129 us (17%)
  blocking collectives  45.8 us (6%)
  matrix products  44.8 us (6%)
  other arithmetic  40.8 us (5%)
  between operations  13.7 us (2%)
    all_gather x1, waiting for transfers between devices, on_device(): piece = lax.all_gather(activations, 'heads', axis=1, tiled=True)  157 us
    psum x1, waiting for transfers between devices, on_device(): shared = lax.psum(chosen_rows.astype(jnp.bfloat16), 'seq')  144 us
    reduce_scatter x1, waiting for transfers between devices, on_device(): lax.psum_scatter(term.astype(jnp.bfloat16), 'heads', scatter_dimension=1,...  137 us
    all_gather x2, blocking collectives, combined_all(): pieces = jax.tree.map(lambda part: lax.all_gather(part, axis), value)  45.8 us
    all_gather x1, waiting for transfers between devices, on_device(): piece = lax.all_gather(stacked, 'seq', axis=1, tiled=True)  45.2 us
    gather x1, local copies, waits for them, and re-layouts, on_device(): chosen = piece[:, jnp.clip(offset_rows, 0, count - 1).reshape(-1)]  37.2 us
    all_gather x1, local copies, waits for them, and re-layouts, on_device(): piece = lax.all_gather(stacked, 'seq', axis=1, tiled=True)  30.9 us
    slice x2, local copies, waits for them, and re-layouts, on_device(): chosen[0]  19.7 us
  transfers between devices with their start and end apart: 7, of which 4 were waited for; matrix products, arithmetic and copies ran while one was open for 8% of the time, Pallas kernels for 0%

commit v1 on v0

--- a/solution.py
+++ b/solution.py
@@ -149,7 +149,7 @@
     chosen_rows = jnp.dot(
         selector.astype(jnp.bfloat16), projected, preferred_element_type=jnp.float32
     )
-    shared = lax.psum(chosen_rows.astype(jnp.bfloat16), "seq")
+    shared = jnp.sum(lax.all_gather(chosen_rows.astype(jnp.bfloat16), "seq"), axis=0)
     g_query = shared[:, :group_width].reshape(global_count, heads_here, head_size)
     g_key = shared[:, group_width : 2 * group_width].reshape(global_count, heads_here, head_size)
     g_value = shared[:, 2 * group_width :].reshape(global_count, heads_here, head_size)

time: 764 us -> 681 us (0.89)
  waiting for transfers between devices: 485 us -> 411 us
    psum x1 -> x0, waiting for transfers between devices: 144 us -> none  [on_device(): shared = lax.psum(chosen_rows.astype(jnp.bfloat16), 'seq')]
    all_gather x0 -> x1, waiting for transfers between devices: none -> 63.6 us  [on_device(): lax.all_gather(chosen_rows.astype(jnp.bfloat16), 'seq')]
  transfers between devices with their start and end apart: 7 -> 7, of which waited for: 4 -> 6; matrix products, arithmetic and copies ran while one was open for 8% -> 8% of each run, Pallas kernels for 0% -> 0%
where the time goes in v1:
time: 681 us; the launch traced here: 679 us
  waiting for transfers between devices  411 us (60%)
  local copies, waits for them, and re-layouts  125 us (18%)
  blocking collectives  44.1 us (6%)
  matrix products  42.9 us (6%)
  other arithmetic  40.7 us (6%)
  between operations  13.6 us (2%)
    all_gather x1, waiting for transfers between devices, on_device(): piece = lax.all_gather(activations, 'heads', axis=1, tiled=True)  157 us
    reduce_scatter x1, waiting for transfers between devices, on_device(): lax.psum_scatter(term.astype(jnp.bfloat16), 'heads', scatter_dimension=1,...  138 us
    all_gather x1, waiting for transfers between devices, on_device(): lax.all_gather(chosen_rows.astype(jnp.bfloat16), 'seq')  63.6 us
    all_gather x1, waiting for transfers between devices, on_device(): piece = lax.all_gather(stacked, 'seq', axis=1, tiled=True)  48.9 us
    all_gather x2, blocking collectives, combined_all(): pieces = jax.tree.map(lambda part: lax.all_gather(part, axis), value)  44.1 us
    gather x1, local copies, waits for them, and re-layouts, on_device(): chosen = piece[:, jnp.clip(offset_rows, 0, count - 1).reshape(-1)]  37.2 us
    all_gather x1, local copies, waits for them, and re-layouts, on_device(): piece = lax.all_gather(stacked, 'seq', axis=1, tiled=True)  30.9 us
    slice x2, local copies, waits for them, and re-layouts, on_device(): chosen[0]  19.8 us
  transfers between devices with their start and end apart: 7, of which 6 were waited for; matrix products, arithmetic and copies ran while one was open for 8% of the time, Pallas kernels for 0%

profile of v1, /device:TPU:1, one launch (start us, length us, event | category | flops | bytes accessed | tf_op | source)
XLA Modules:
  0.0 678.6 jit_solution(6983713132792704041)
XLA Ops:
  8.0 157.4 %all-gather.11.cloned.1.call-done = bf16[768,4096]{1,0:T(8,128)(2,1)} async-done(((bf16[768,256]{1,0:T(8,128)(2,1)}), bf16[768,4096]{1,0:T(8,128)(2,1)}) %all-gather.11.cloned.1.call-update) | async-done | bytes 6291472 | tf_op jit(solution)/shard_map/all_gather | solution.py:71
  165.4 5.4 convolution_convert_fusion.1
  177.2 63.6 %all-gather.15.cloned.1.call-done = bf16[2048,768]{1,0:T(8,128)(2,1)} async-done(((bf16[128,768]{1,0:T(8,128)(2,1)}), bf16[2048,768]{1,0:T(8,128)(2,1)}) %all-gather.15.cloned.1.call-update) | async-done | bytes 3145744 | tf_op jit(solution)/shard_map/all_gather | solution.py:152
  256.2 2.7 collective-permute-done.1
  261.0 2.4 copy.143
  263.4 3.0 reshape.310
  270.0 4.7 fusion.91
  277.0 2.7 fusion.8
  280.2 24.4 %all-gather.5 = f32[16,2,128]{2,1,0:T(2,128)S(1)} all-gather(f32[1,2,128]{2,1,0:T(2,128)S(1)} %bitcast.212), channel_id=4, replica_groups=mesh['seq'=16,'heads'=16] {'seq'}, dimensions={0}, use_global_device_ids=true | all-gather | bytes 17408 | tf_op jit(solution)/shard_map/all_gather | solution.py:26
  304.7 19.6 %all-gather.4 = f32[16,2,128]{2,1,0:T(2,128)S(1)} all-gather(f32[1,2,128]{2,1,0:T(2,128)S(1)} %bitcast.211), channel_id=3, replica_groups=mesh['seq'=16,'heads'=16] {'seq'}, dimensions={0}, use_global_device_ids=true | all-gather | bytes 17408 | tf_op jit(solution)/shard_map/all_gather | solution.py:26
  325.5 3.1 slice.104
  328.6 16.8 %while.14 = (s32[]{:T(128)}, f32[2,128]{1,0:T(2,128)S(1)}, f32[2,128]{1,0:T(2,128)S(1)}, f32[2,128,128]{2,1,0:T(8,128)S(1)}, f32[15,2,128]{2,1,0:T(2,128)S(1)}, ...) while((s32[]{:T(128)}, f32[2,128]{1,0:T(2,128)S(1)}, f32[2,128]{1,0:T(2,128)S(1)}, ...), condition=%wide.region_5.6_spmd, body=%wide.region_4.5_spmd.sunk | while | flops 99842 | bytes 403557 | solution.py:29
  345.6 48.9 %all-gather.13.cloned.1.call-done = bf16[2,12288,256]{1,2,0:T(8,128)(2,1)} async-done(((bf16[2,768,256]{1,2,0:T(8,128)(2,1)}), bf16[2,12288,256]{1,2,0:T(8,128)(2,1)}) %all-gather.13.cloned.1.call-update) | async-done | bytes 12582928 | tf_op jit(solution)/shard_map/all_gather | solution.py:122
  394.5 30.9 %copy.151 = bf16[2,12288,256]{2,0,1:T(2,128)(2,1)} copy(bf16[2,12288,256]{1,2,0:T(8,128)(2,1)} %all-gather.13.cloned.1.call-done) | data formatting | bytes 25165824 | tf_op jit(solution)/shard_map/all_gather | solution.py:122
  425.4 37.2 %gather_fusion.1 = bf16[4096,2,256]{2,1,0:T(2,128)(2,1)} fusion(bf16[2,12288,256]{2,0,1:T(2,128)(2,1)} %copy.151, s32[4096]{0:T(1024)S(1)} %copy-done.11), kind=kCustom, calls=%fused_computation.1 | custom fusion | bytes 8404992 | tf_op jit(solution)/shard_map/gather | solution.py:128
  462.6 10.1 %fusion.90 = (bf16[1,4096,256]{2,0,1:T(2,128)(2,1)}, bf16[1,4096,256]{2,0,1:T(2,128)(2,1)}) fusion(bf16[2,4096,256]{2,0,1:T(2,128)(2,1)} %bitcast.184), kind=kLoop, calls=%fused_computation.145 | loop fusion | bytes 8388608 | tf_op jit(solution)/shard_map/slice | solution.py:131
  472.6 9.8 %copy.152 = bf16[1,4096,256]{1,2,0:T(8,128)(2,1)} copy(bf16[1,4096,256]{2,0,1:T(2,128)(2,1)} %get-tuple-element.72) | data formatting | bytes 4194304 | tf_op jit(solution)/shard_map/slice | solution.py:131
  482.4 9.8 %copy.161 = bf16[1,4096,256]{1,2,0:T(8,128)(2,1)} copy(bf16[1,4096,256]{2,0,1:T(2,128)(2,1)} %get-tuple-element.73) | data formatting | bytes 4194304 | tf_op jit(solution)/shard_map/slice | solution.py:141
  492.2 7.7 %fusion.3 = (f32[6,2,128]{2,0,1:T(8,128)S(1)}, f32[2,4096,6,128]{3,1,2,0:T(8,128)S(1)}) fusion(pred[6,4096]{1,0:T(8,128)(4,1)S(1)} %bitcast.202, bf16[4096,2,128,1]{0,2,3,1:T(8,128)(2,1)} %bitcast.197, bf16[6,128,2,128]{3,2,1,0:T(2,128)(2,1)S(1)} %copy-done.4), kind=kOutput, calls=%fused_computation.13 | convolution fusion | flops 1629485568 | bytes 27686912 | tf_op jit(solution)/shard_map/bqhd,khd->bhqk/dot_general | solution.py:131
  501.3 13.5 %fusion.4 = (f32[6,2,128]{2,0,1:T(8,128)S(1)}, bf16[6,2,128,4096]{2,3,0,1:T(8,128)(2,1)}) fusion(f32[2,4096,6,128]{3,1,2,0:T(8,128)S(1)} %get-tuple-element.89, f32[6,2,128]{2,0,1:T(8,128)S(1)} %copy.163, pred[6,4096]{1,0:T(8,128)(4,1)S(1)} %bitcast.203), kind=kLoop, calls=%fused_computation.14 | loop fusion | flops 37747200 | bytes 37785600 | tf_op jit(solution)/shard_map/reduce_sum | solution.py:41
  514.8 10.6 %fusion.18 = f32[6,128,2,128]{3,1,2,0:T(8,128)} fusion(bf16[4096,2,128,1]{0,2,1,3:T(8,128)(2,1)S(1)} %bitcast.196, bf16[6,2,128,4096]{2,3,0,1:T(8,128)(2,1)} %get-tuple-element.71), kind=kOutput, calls=%fused_computation.31 | convolution fusion | flops 1610612736 | bytes 15466496 | tf_op jit(solution)/shard_map/bhqk,khd->bhqd/dot_general | solution.py:141
  525.4 3.2 fusion.33
  530.1 4.5 convolution_convert_fusion
  534.6 137.5 %reduce-scatter.2.cloned.1.call-done = bf16[768,256]{1,0:T(8,128)(2,1)} async-done(((bf16[768,4096]{1,0:T(8,128)(2,1)}), bf16[768,256]{1,0:T(8,128)(2,1)}) %reduce-scatter.2.cloned.1.call-update) | async-done | bytes 393232 | tf_op jit(solution)/shard_map/reduce_scatter | solution.py:191
  (161 shorter events, 52.2 us)
Async XLA Ops:
  6.5 523.5 %copy-start = (bf16[256,4096]{1,0:T(8,128)(2,1)S(1)}, bf16[256,4096]{1,0:T(8,128)(2,1)}, u32[]{:S(2)}) copy-start(bf16[256,4096]{1,0:T(8,128)(2,1)} %param.14) | copy-start | bytes 6291460
  6.5 158.8 %all-gather.11.cloned.1.call-start = ((), (), s32[]{:S(2)}) async-start(), calls=%async_computation.1 | async-start | bytes 6684672 | tf_op jit(solution)/shard_map/all_gather | solution.py:71
  7.3 233.6 %all-gather.15.cloned.1.call-start = ((), (), s32[]{:S(2)}) async-start(), calls=%async_computation.4 | async-start | bytes 3342336 | tf_op jit(solution)/shard_map/all_gather | solution.py:152
  8.0 241.7 %copy-start.13 = (s32[128]{0:T(128)}, s32[128]{0:T(128)S(1)}, u32[]{:S(2)}) copy-start(s32[128]{0:T(128)S(1)} %get-tuple-element.69) | copy-start | bytes 1540
  165.4 5.4 copy-start.16
  165.4 5.8 copy-start.17
  171.2 2.0 copy-start.18
  177.2 148.3 %all-gather.17.cloned.1.call-start = ((), (), s32[]{:S(2)}) async-start(), calls=%async_computation.5 | async-start | bytes 2228224 | tf_op jit(solution)/shard_map/all_gather | solution.py:26
  240.9 6.6 copy-start.12
  243.2 6.6 copy-start.19
  246.4 148.1 %all-gather.13.cloned.1.call-start = ((), (), s32[]{:S(2)}) async-start(), calls=%async_computation.2 | async-start | bytes 13369344 | tf_op jit(solution)/shard_map/all_gather | solution.py:122
  247.4 424.7 %reduce-scatter.2.cloned.1.call-start = ((), (), s32[]{:S(2)}) async-start(), calls=%async_computation.3 | async-start | bytes 6684672 | tf_op jit(solution)/shard_map/reduce_scatter | solution.py:191
  251.5 4.7 collective-permute-start
  252.5 6.3 collective-permute-start.1
  274.6 2.4 copy-start.4
  277.0 2.8 copy-start.9
  277.0 2.9 copy-start.8
  277.0 3.0 copy-start.3
  325.5 3.1 slice-start
  345.6 79.8 %copy-start.11 = (s32[4096]{0:T(1024)S(1)}, s32[4096]{0:T(1024)}, u32[]{:S(2)}) copy-start(s32[4096]{0:T(1024)} %broadcast_clamp_fusion) | copy-start | bytes 49156
  482.4 9.8 %copy-start.10 = (pred[1,6,32,128]{3,1,2,0:T(8,128)(4,1)S(1)}, pred[1,6,32,128]{3,1,2,0:T(8,128)(4,1)}, u32[]{:S(2)}) copy-start(pred[1,6,32,128]{3,1,2,0:T(8,128)(4,1)} %copy.225) | copy-start | bytes 73732
  492.2 7.7 %copy-start.5 = (f32[6,2,128,128]{2,3,0,1:T(8,128)S(1)}, f32[6,2,128,128]{2,3,0,1:T(8,128)}, u32[]{:S(2)}) copy-start(f32[6,2,128,128]{2,3,0,1:T(8,128)} %get-tuple-element.87) | copy-start | bytes 2359300
  492.2 7.9 %copy-start.1 = (f32[6,2,128,640]{3,2,1,0:T(8,128)S(1)}, f32[6,2,128,640]{3,2,1,0:T(8,128)}, u32[]{:S(2)}) copy-start(f32[6,2,128,640]{3,2,1,0:T(8,128)} %get-tuple-element.91) | copy-start | bytes 11796484
  501.3 13.5 %copy-start.6 = (bf16[1,4096,256]{1,2,0:T(8,128)(2,1)S(1)}, bf16[1,4096,256]{1,2,0:T(8,128)(2,1)}, u32[]{:S(2)}) copy-start(bf16[1,4096,256]{1,2,0:T(8,128)(2,1)} %copy.161) | copy-start | bytes 6291460
  (4 other events, 3.3 us)
Sparse Core Ops, SparseCore 0:
  9.1 156.2 all-gather.10
  177.3 63.5 all-gather.14
  246.5 51.4 all-gather.16
  300.6 93.8 all-gather.12
  534.7 137.3 reduce-scatter.1
